TPU v7x, 32 devices: a whole 2x2x4 slice. The times are simulated.
32 devices in a mesh: groups: 2 (over y), freq: 4 (over z), space: 2 (over x), blk: 2 (over core).
Axes of the slice: x: 2, y: 2, z: 4, core: 2. Of those that a mesh axis runs over, the one named last changes fastest.
Arguments:
- realizations: bfloat16 [16, 64, 2, 8192], P('freq', 'groups', None, ('space', 'blk')), parts along dimension 1, may hold values from -6 to 6
- weights: float32 [16384], P(('groups', 'space', 'blk')), parts along dimension 0, may hold values from 0.25 to 4
- partners: int32 [3, 4], replicated, may hold values from 0 to 3, each once within a row
- block_count: int32 [2], P('groups'), parts along dimension 0, may hold values from 16 to 32
Outputs:
- modes: bfloat16 [16, 64, 2, 8192], P('freq', 'groups', None, ('space', 'blk')), parts along dimension 1
- gram: float32 [6, 16, 4, 2, 32, 32], P('groups', 'freq'), parts along dimension 0
There are 2 independent parts, one for each index of `groups`. A program takes and returns all parts, laid end to end along the dimension named above; an argument that names none is the same for every part. Nothing has to cross between parts.
Inputs may be any that keep to these rules, and one draw needn't show every extreme that they name: `partners`: each row is a permutation of the groups 0 to 3. `block_count`: blocks from this index on are left out.
All inputs are finite; a program needn't handle non-finite values.
Results may differ from a plain program's by a relative error of at most 0.0057.
Values may be sent and summed in bfloat16 or wider, within the bound.
A program may use at most 128 MiB of HBM per device.

v0:
```python
import jax
import jax.numpy as jnp
from jax import lax
from jax.sharding import PartitionSpec as P


def round_tables(partners, group_index, own_rows, which_round, per_group, total_freqs):
    offsets = jnp.arange(per_group, dtype=jnp.int32)
    partner_idx = partners[which_round, group_index] * per_group + offsets
    target_idx = (own_rows[:, None] + partner_idx[None, :]) % total_freqs
    return (partner_idx, target_idx)


def body(realizations, weights, partners, block_count):
    per_group = realizations.shape[0]
    blocks = realizations.shape[1]
    points = realizations.shape[3]
    rounds = partners.shape[0]
    shard_count = lax.axis_size("freq")
    total_freqs = per_group * shard_count
    total_space = points * lax.axis_size("space") * lax.axis_size("blk")
    gram_scale = 1.0 / jnp.sqrt(jnp.float32(total_space))
    mode_scale = 1.0 / jnp.sqrt(jnp.float32(rounds * per_group * blocks))
    keeper = (jnp.arange(blocks, dtype=jnp.int32) < block_count[0]).astype(jnp.bfloat16)
    fields = realizations * keeper[None, :, None, None]
    gathered = lax.all_gather(fields, "freq", axis=0, tiled=True)
    group_index = lax.axis_index("freq")
    own_rows = group_index * per_group + jnp.arange(per_group, dtype=jnp.int32)
    first = fields.astype(jnp.float32)[:, None]
    first_real = first[:, :, :, 0]
    first_imag = first[:, :, :, 1]
    round_grams = []
    for which_round in range(rounds):
        partner_idx, target_idx = round_tables(
            partners, group_index, own_rows, which_round, per_group, total_freqs
        )
        second = gathered[partner_idx].astype(jnp.float32)[None]
        real_part = first_real * second[:, :, :, 0] - first_imag * second[:, :, :, 1]
        imag_part = first_real * second[:, :, :, 1] + first_imag * second[:, :, :, 0]
        prod_real = (real_part * weights).astype(jnp.bfloat16)
        prod_imag = (imag_part * weights).astype(jnp.bfloat16)
        targets = gathered[target_idx]
        target_real = targets[:, :, :, 0]
        target_imag = targets[:, :, :, 1]
        real_gram = jnp.einsum(
            "ijas,ijbs->ijab", prod_real, target_real, preferred_element_type=jnp.float32
        ) + jnp.einsum(
            "ijas,ijbs->ijab", prod_imag, target_imag, preferred_element_type=jnp.float32
        )
        imag_gram = jnp.einsum(
            "ijas,ijbs->ijab", prod_real, target_imag, preferred_element_type=jnp.float32
        ) - jnp.einsum(
            "ijas,ijbs->ijab", prod_imag, target_real, preferred_element_type=jnp.float32
        )
        round_grams.append(jnp.stack([real_gram, imag_gram], axis=2))
    partial_value = jnp.stack(round_grams, axis=0)
    grams = lax.psum(partial_value, ("space", "blk")) * gram_scale
    accumulated = None
    for which_round in range(rounds):
        partner_idx, target_idx = round_tables(
            partners, group_index, own_rows, which_round, per_group, total_freqs
        )
        targets = gathered[target_idx]
        target_real = targets[:, :, :, 0]
        target_imag = targets[:, :, :, 1]
        rounded = grams[which_round].astype(jnp.bfloat16)
        real_mode = jnp.einsum(
            "ijab,ijbs->ias", rounded[:, :, 0], target_real, preferred_element_type=jnp.float32
        ) - jnp.einsum(
            "ijab,ijbs->ias", rounded[:, :, 1], target_imag, preferred_element_type=jnp.float32
        )
        imag_mode = jnp.einsum(
            "ijab,ijbs->ias", rounded[:, :, 0], target_imag, preferred_element_type=jnp.float32
        ) + jnp.einsum(
            "ijab,ijbs->ias", rounded[:, :, 1], target_real, preferred_element_type=jnp.float32
        )
        term = jnp.stack([real_mode, imag_mode], axis=2)
        accumulated = term if accumulated is None else accumulated + term
    modes = (accumulated * mode_scale).astype(jnp.bfloat16)
    return (modes, grams)


def solution(mesh):
    placed = (
        P("freq", "groups", None, ("space", "blk")),
        P(("groups", "space", "blk")),
        P(),
        P("groups"),
    )
    return jax.shard_map(
        body,
        mesh=mesh,
        in_specs=placed,
        out_specs=(
            P("freq", "groups", None, ("space", "blk")),
            P("groups", "freq", None, None, None, None),
        ),
        check_vma=False,
    )
```

profile of v0, /device:TPU:0, one launch (start us, length us, event | category | flops | bytes accessed | tf_op | source)
XLA Modules:
  0.0 216.9 jit_solution(5189849193543373611)
XLA Ops:
  7.9 2.8 %bitcast_convert_fusion.3 = (f32[4,1,32,2,2048]{4,2,3,0,1:T(8,128)S(1)}, bf16[4,32,2,2048]{3,1,2,0:T(8,128)(2,1)}) fusion(bf16[32]{0:T(256)(128)(2,1)S(1)} %compare_convert_fusion, bf16[4,32,2,2048]{3,2,1,0:T(2,128)(2,1)} %param.4), kind=kLoop, calls=%fused_computation.142 | loop fusion | flops 1048576 | bytes 4194368 | tf_op jit(solution)/shard_map/broadcast_in_dim | solution.py:29
  10.8 0.7 constant_dynamic-slice_fusion.1
  13.9 1.2 slice_bitcast_fusion.61
  15.1 79.3 %all-gather.2.cloned.1.call-done = bf16[16,32,2,2048]{3,1,2,0:T(8,128)(2,1)} async-done(((bf16[4,32,2,2048]{3,1,2,0:T(8,128)(2,1)}), bf16[16,32,2,2048]{3,1,2,0:T(8,128)(2,1)}) %all-gather.2.cloned.1.call-update) | async-done | bytes 4194320 | tf_op jit(solution)/shard_map/all_gather | solution.py:26
  94.4 2.8 %gather_fusion.4 = bf16[4,32,2,2048]{3,1,2,0:T(8,128)(2,1)S(1)} fusion(bf16[16,32,2,2048]{3,1,2,0:T(8,128)(2,1)} %all-gather.2.cloned.1.call-done, s32[1024]{0:T(1024)S(1)} %pad_clamp_fusion.1), kind=kCustom, calls=%fused_computation.4 | custom fusion | bytes 2097168 | tf_op jit(solution)/shard_map/gather | solution.py:37
  97.4 1.2 slice_bitcast_fusion.55
  98.6 5.4 %gather_fusion.5 = bf16[16,32,2,2048]{3,1,2,0:T(8,128)(2,1)} fusion(bf16[16,32,2,2048]{3,1,2,0:T(8,128)(2,1)} %all-gather.2.cloned.1.call-done, s32[1024]{0:T(1024)S(1)} %pad_clamp_fusion), kind=kCustom, calls=%fused_computation.5 | custom fusion | bytes 8388672 | tf_op jit(solution)/shard_map/gather | solution.py:42
  104.0 2.6 %copy.14 = bf16[16,32,2,2048]{3,1,0,2:T(8,128)(2,1)S(1)} copy(bf16[16,32,2,2048]{3,1,2,0:T(8,128)(2,1)} %gather_fusion.5) | data formatting | bytes 8388608 | tf_op jit(solution)/shard_map/gather | solution.py:42
  106.8 1.9 fusion.20
  108.7 1.2 fusion.21
  109.9 2.8 %gather_fusion.2 = bf16[4,32,2,2048]{3,1,2,0:T(8,128)(2,1)S(1)} fusion(bf16[16,32,2,2048]{3,1,2,0:T(8,128)(2,1)} %all-gather.2.cloned.1.call-done, s32[1024]{0:T(1024)S(1)} %pad_clamp_fusion.3), kind=kCustom, calls=%fused_computation.2 | custom fusion | bytes 2097168 | tf_op jit(solution)/shard_map/gather | solution.py:37
  113.0 1.2 slice_bitcast_fusion.57
  114.2 5.4 %gather_fusion.3 = bf16[16,32,2,2048]{3,1,2,0:T(8,128)(2,1)} fusion(bf16[16,32,2,2048]{3,1,2,0:T(8,128)(2,1)} %all-gather.2.cloned.1.call-done, s32[1024]{0:T(1024)S(1)} %pad_clamp_fusion.2), kind=kCustom, calls=%fused_computation.3 | custom fusion | bytes 8388672 | tf_op jit(solution)/shard_map/gather | solution.py:42
  119.6 2.6 %copy.13 = bf16[16,32,2,2048]{3,1,0,2:T(8,128)(2,1)S(1)} copy(bf16[16,32,2,2048]{3,1,2,0:T(8,128)(2,1)} %gather_fusion.3) | data formatting | bytes 8388608 | tf_op jit(solution)/shard_map/gather | solution.py:42
  122.2 2.0 fusion.16
  124.2 1.9 fusion.17
  126.1 2.8 %gather_fusion = bf16[4,32,2,2048]{3,1,2,0:T(8,128)(2,1)S(1)} fusion(bf16[16,32,2,2048]{3,1,2,0:T(8,128)(2,1)} %all-gather.2.cloned.1.call-done, s32[1024]{0:T(1024)S(1)} %pad_clamp_fusion.5), kind=kCustom, calls=%fused_computation | custom fusion | bytes 2097168 | tf_op jit(solution)/shard_map/gather | solution.py:37
  129.2 1.2 slice_bitcast_fusion.60
  130.4 4.9 %gather_fusion.1 = bf16[16,32,2,2048]{3,1,2,0:T(8,128)(2,1)} fusion(bf16[16,32,2,2048]{3,1,2,0:T(8,128)(2,1)} %all-gather.2.cloned.1.call-done, s32[1024]{0:T(1024)S(1)} %pad_clamp_fusion.4), kind=kCustom, calls=%fused_computation.1 | custom fusion | bytes 8388672 | tf_op jit(solution)/shard_map/gather | solution.py:42
  135.3 2.6 %copy.12 = bf16[16,32,2,2048]{3,1,0,2:T(8,128)(2,1)S(1)} copy(bf16[16,32,2,2048]{3,1,2,0:T(8,128)(2,1)} %gather_fusion.1) | data formatting | bytes 8388608 | tf_op jit(solution)/shard_map/gather | solution.py:42
  137.9 1.2 fusion.12
  139.2 1.2 fusion.13
  140.4 1.1 copy-done.1
  142.1 1.4 fusion.90
  143.6 1.7 fusion.88
  146.4 1.3 fusion.94
  147.7 1.9 fusion.92
  149.6 1.2 fusion.98
  150.8 1.6 fusion.96
  152.6 1.4 pad_maximum_fusion
  154.0 41.5 %all-reduce.2.cloned.1.call-done = f32[3,4,4,2,32,32]{5,4,2,1,3,0:T(8,128)} async-done(((f32[3,4,4,2,32,32]{5,4,2,1,3,0:T(8,128)}), f32[3,4,4,2,32,32]{5,4,2,1,3,0:T(8,128)}) %all-reduce.2.cloned.1.call-update) | async-done | bytes 393232 | tf_op jit(solution)/shard_map/psum | solution.py:57
  195.5 1.8 broadcast_multiply_fusion
  197.4 0.7 copy-done.2
  198.1 0.6 convolution_bitcast_fusion
  198.7 0.6 convolution_bitcast_fusion.2
  199.7 0.6 convolution_bitcast_fusion.4
  200.3 0.6 convolution_bitcast_fusion.6
  201.2 0.6 convolution_bitcast_fusion.8
  201.8 0.6 convolution_bitcast_fusion.10
  202.4 1.3 copy.16
  203.7 0.6 fusion.11
  204.3 0.6 fusion.9
  204.9 0.6 fusion.7
  205.5 0.6 fusion.5
  206.1 0.6 fusion.3
  206.7 0.6 fusion.1
  207.3 0.7 fusion.26
  208.0 2.0 copy.15
  (71 shorter events, 4.0 us)
Async XLA Ops:
  7.2 3.6 %copy-start.18 = (s32[3,4]{1,0:T(4,128)S(1)}, s32[3,4]{1,0:T(4,128)}, u32[]{:S(2)}) copy-start(s32[3,4]{1,0:T(4,128)} %param.6) | copy-start | bytes 148
  7.2 87.2 %all-gather.2.cloned.1.call-start = ((), (), s32[]{:S(2)}) async-start(), calls=%async_computation | async-start | bytes 5242880 | tf_op jit(solution)/shard_map/all_gather | solution.py:26
  10.8 184.7 %all-reduce.2.cloned.1.call-start = ((), (), s32[]{:S(2)}) async-start(), calls=%async_computation.1 | async-start | bytes 3145728 | tf_op jit(solution)/shard_map/psum | solution.py:57
  98.6 10.1 %copy-start.9 = (f32[4,32,2048]{2,1,0:T(8,128)}, f32[4,32,2048]{2,1,0:T(8,128)S(1)}, u32[]{:S(2)}) copy-start(f32[4,32,2048]{2,1,0:T(8,128)S(1)} %get-tuple-element.14) | copy-start | bytes 3145732
  104.0 2.7 %copy-start.8 = (f32[4,32,2048]{2,1,0:T(8,128)S(1)}, f32[4,32,2048]{2,1,0:T(8,128)}, u32[]{:S(2)}) copy-start(f32[4,32,2048]{2,1,0:T(8,128)} %get-tuple-element.13) | copy-start | bytes 3145732
  104.0 2.8 %copy-start.11 = (f32[4,32,2048]{2,1,0:T(8,128)S(1)}, f32[4,32,2048]{2,1,0:T(8,128)}, u32[]{:S(2)}) copy-start(f32[4,32,2048]{2,1,0:T(8,128)} %get-tuple-element.15) | copy-start | bytes 3145732
  104.0 2.8 %copy-start.19 = (f32[2048]{0:T(1024)S(1)}, f32[2048]{0:T(1024)}, u32[]{:S(2)}) copy-start(f32[2048]{0:T(1024)} %param.5) | copy-start | bytes 24580
  106.6 2.1 copy-start
  114.2 10.0 %copy-start.13 = (f32[4,32,2048]{2,1,0:T(8,128)}, f32[4,32,2048]{2,1,0:T(8,128)S(1)}, u32[]{:S(2)}) copy-start(f32[4,32,2048]{2,1,0:T(8,128)S(1)} %get-tuple-element.10) | copy-start | bytes 3145732
  119.5 2.6 %copy-start.15 = (f32[4,32,2048]{2,1,0:T(8,128)S(1)}, f32[4,32,2048]{2,1,0:T(8,128)}, u32[]{:S(2)}) copy-start(f32[4,32,2048]{2,1,0:T(8,128)} %get-tuple-element.11) | copy-start | bytes 3145732
  122.1 2.1 copy-start.3
  135.3 2.6 %copy-start.17 = (f32[4,32,2048]{2,1,0:T(8,128)S(1)}, f32[4,32,2048]{2,1,0:T(8,128)}, u32[]{:S(2)}) copy-start(f32[4,32,2048]{2,1,0:T(8,128)} %get-tuple-element.9) | copy-start | bytes 3145732
  137.9 12.9 %copy-start.6 = (bf16[16,32,2,2048]{3,1,0,2:T(8,128)(2,1)}, bf16[16,32,2,2048]{3,1,0,2:T(8,128)(2,1)S(1)}, u32[]{:S(2)}) copy-start(bf16[16,32,2,2048]{3,1,0,2:T(8,128)(2,1)S(1)} %copy.12) | copy-start | bytes 12582916
  139.2 2.4 %copy-start.1 = (bf16[16,32,2,2048]{3,1,0,2:T(8,128)(2,1)S(1)}, bf16[16,32,2,2048]{3,1,0,2:T(8,128)(2,1)}, u32[]{:S(2)}) copy-start(bf16[16,32,2,2048]{3,1,0,2:T(8,128)(2,1)} %copy-done) | copy-start | bytes 12582916
  139.2 2.6 %copy-start.10 = (f32[4,32,2048]{2,1,0:T(8,128)S(1)}, f32[4,32,2048]{2,1,0:T(8,128)}, u32[]{:S(2)}) copy-start(f32[4,32,2048]{2,1,0:T(8,128)} %copy-done.9) | copy-start | bytes 3145732
  139.2 3.0 %copy-start.12 = (f32[4,32,2048]{2,1,0:T(8,128)S(1)}, f32[4,32,2048]{2,1,0:T(8,128)}, u32[]{:S(2)}) copy-start(f32[4,32,2048]{2,1,0:T(8,128)} %get-tuple-element.15) | copy-start | bytes 3145732
  139.2 3.0 %copy-start.20 = (f32[4,4,32,32]{3,2,1,0:T(8,128)S(1)}, f32[4,4,32,32]{3,2,1,0:T(8,128)}, u32[]{:S(2)}) copy-start(f32[4,4,32,32]{3,2,1,0:T(8,128)} %fusion.20) | copy-start | bytes 196612
  143.5 2.2 %copy-start.4 = (bf16[16,32,2,2048]{3,1,0,2:T(8,128)(2,1)S(1)}, bf16[16,32,2,2048]{3,1,0,2:T(8,128)(2,1)}, u32[]{:S(2)}) copy-start(bf16[16,32,2,2048]{3,1,0,2:T(8,128)(2,1)} %copy-done.3) | copy-start | bytes 12582916
  143.5 2.5 %copy-start.14 = (f32[4,32,2048]{2,1,0:T(8,128)S(1)}, f32[4,32,2048]{2,1,0:T(8,128)}, u32[]{:S(2)}) copy-start(f32[4,32,2048]{2,1,0:T(8,128)} %copy-done.13) | copy-start | bytes 3145732
  143.6 2.8 %copy-start.16 = (f32[4,32,2048]{2,1,0:T(8,128)S(1)}, f32[4,32,2048]{2,1,0:T(8,128)}, u32[]{:S(2)}) copy-start(f32[4,32,2048]{2,1,0:T(8,128)} %get-tuple-element.11) | copy-start | bytes 3145732
  143.6 2.8 %copy-start.22 = (f32[4,4,32,32]{3,2,1,0:T(8,128)S(1)}, f32[4,4,32,32]{3,2,1,0:T(8,128)}, u32[]{:S(2)}) copy-start(f32[4,4,32,32]{3,2,1,0:T(8,128)} %fusion.16) | copy-start | bytes 196612
  146.4 1.3 copy-start.21
  195.5 2.7 %copy-start.2 = (bf16[16,32,2,2048]{3,1,0,2:T(8,128)(2,1)S(1)}, bf16[16,32,2,2048]{3,1,0,2:T(8,128)(2,1)}, u32[]{:S(2)}) copy-start(bf16[16,32,2,2048]{3,1,0,2:T(8,128)(2,1)} %copy-done) | copy-start | bytes 12582916
  197.3 2.4 %copy-start.5 = (bf16[16,32,2,2048]{3,1,0,2:T(8,128)(2,1)S(1)}, bf16[16,32,2,2048]{3,1,0,2:T(8,128)(2,1)}, u32[]{:S(2)}) copy-start(bf16[16,32,2,2048]{3,1,0,2:T(8,128)(2,1)} %copy-done.3) | copy-start | bytes 12582916
  198.7 2.4 %copy-start.7 = (bf16[16,32,2,2048]{3,1,0,2:T(8,128)(2,1)S(1)}, bf16[16,32,2,2048]{3,1,0,2:T(8,128)(2,1)}, u32[]{:S(2)}) copy-start(bf16[16,32,2,2048]{3,1,0,2:T(8,128)(2,1)} %copy-done.6) | copy-start | bytes 12582916
Sparse Core Ops, SparseCore 0:
  10.9 83.4 all-gather.1
  154.1 41.3 all-reduce.1
where the time goes:
time: 217 us
  waiting for transfers between devices  121 us (56%)
  local copies, waits for them, and re-layouts  45.3 us (21%)
  matrix products  25.9 us (12%)
  between operations  17 us (8%)
  other arithmetic  7.77 us (4%)
    all_gather x1, waiting for transfers between devices, body(): gathered = lax.all_gather(fields, 'freq', axis=0, tiled=True)  79.3 us
    psum x1, waiting for transfers between devices, body(): grams = lax.psum(partial_value, ('space', 'blk')) * gram_scale  41.5 us
    gather x6, local copies, waits for them, and re-layouts, body(): targets = gathered[target_idx]  23.5 us
    gather x3, local copies, waits for them, and re-layouts, body(): second = gathered[partner_idx].astype(jnp.float32)[None]  8.4 us
    unnamed x48, local copies, waits for them, and re-layouts  7.75 us
    dot_general x3, matrix products, body(): jnp.einsum('ijas,ijbs->ijab', prod_real, target_imag, preferred_element_t...  5.19 us
    dot_general x3, matrix products, body(): jnp.einsum('ijas,ijbs->ijab', prod_imag, target_imag, preferred_element_t...  5.13 us
    mul x4, local copies, waits for them, and re-layouts, body(): first_real * second[:, :, :, 0] - first_imag * second[:, :, :, 1]  4.69 us
  transfers between devices with their start and end apart: 2, of which 2 were waited for; matrix products, arithmetic and copies ran while one was open for 1% of the time, Pallas kernels for 0%

commit v1 on v0

v1 whole, which is shorter than its diff:
```python
import functools
import math

import jax
import jax.numpy as jnp
from jax import lax
from jax.experimental import pallas as pl
from jax.experimental.pallas import tpu as pltpu
from jax.sharding import PartitionSpec as P

MESH = pl.DeviceIdType.MESH
F32 = jnp.float32
BF16 = jnp.bfloat16
AXES = ("freq", "space", "blk")


def kernel(dims, partners_ref, x_ref, w_ref, out_ref, gram_ref,
           q, wq, sec, prod, gf, r1, b2, r2, b3, r3, gfull, mo,
           own_sem, in_s, in_r, c_s, c_r, x_s, x_r, z_s, z_r,
           gz_s, gz_r, gx_s, gx_r, gc_s, gc_r, out_s, out_r):
    nz, nx, nc, rounds, per, nb, pts, gram_scale, mode_scale = dims
    width = per * nb
    rows = per * 2 * nb
    half = rows // nc
    part = half // nx
    freqs = nz * per
    z = lax.axis_index("freq")
    x = lax.axis_index("space")
    c = lax.axis_index("blk")

    def peer(me, d, n):
        return lax.rem(me + d, n)

    barrier = pltpu.get_barrier_semaphore()
    for name, me, n in (("freq", z, nz), ("space", x, nx), ("blk", c, nc)):
        for d in range(1, n):
            pl.semaphore_signal(barrier, inc=1, device_id={name: peer(me, d, n)}, device_id_type=MESH)
    pl.semaphore_wait(barrier, nz + nx + nc - 3)

    def remote(src, dst, send, recv, name, to):
        copy = pltpu.make_async_remote_copy(
            src_ref=src, dst_ref=dst, send_sem=send, recv_sem=recv,
            device_id={name: to}, device_id_type=MESH)
        copy.start()
        return copy

    incoming = []
    mine = pl.ds(z * per, per)
    for d in range(nz - 1, 0, -1):
        to = peer(z, d, nz)
        incoming.append(remote(x_ref.at[to], q.at[:, mine], in_s.at[d], in_r.at[d], "freq", to))
    own = pltpu.make_async_copy(x_ref.at[z], q.at[:, mine], own_sem)
    own.start()
    own.wait()
    for copy in incoming:
        copy.wait_recv()

    weights = w_ref[pl.ds(z, 1), :]

    def weigh(f, carry):
        wq[0, f] = q[0, f].astype(F32) * weights
        wq[1, f] = q[1, f].astype(F32) * weights
        return carry

    lax.fori_loop(0, freqs, weigh, 0)

    lane_j = lax.broadcasted_iota(jnp.int32, (nb, width), 1) // nb

    def targets(g, p, i):
        at = [lax.rem((g + p) * per + i + j, freqs) for j in range(per)]
        return jnp.concatenate([q[h, t] for h in range(2) for t in at], axis=0)

    def grams(r):
        def group(g, carry):
            p = partners_ref[r, g]
            for h in range(2):
                for j in range(per):
                    sec[h, j] = q[h, p * per + j].astype(F32)

            def one(i, inner):
                first_re = wq[0, g * per + i]
                first_im = wq[1, g * per + i]
                for j in range(per):
                    second_re = sec[0, j]
                    second_im = sec[1, j]
                    prod[pl.ds(j * nb, nb), :] = (first_re * second_re - first_im * second_im).astype(BF16)
                    prod[pl.ds(width + j * nb, nb), :] = (first_re * second_im + first_im * second_re).astype(BF16)
                full = lax.dot_general(prod[...], targets(g, p, i), (((1,), (1,)), ((), ())),
                                       preferred_element_type=F32)
                g_re = full[:width, :width] + full[width:, width:]
                g_im = full[:width, width:] - full[width:, :width]
                re, im = g_re[:nb], g_im[:nb]
                for j in range(1, per):
                    keep = lane_j == j
                    re = jnp.where(keep, g_re[j * nb:(j + 1) * nb], re)
                    im = jnp.where(keep, g_im[j * nb:(j + 1) * nb], im)
                base = pl.multiple_of(i * 2 * nb, 2 * nb)
                gf[r, g, pl.ds(base, 2 * nb), :] = jnp.concatenate([re, im], axis=0)
                return inner

            return lax.fori_loop(0, per, one, carry)

        lax.fori_loop(0, nz, group, 0)

    half_at = pl.ds(pl.multiple_of(c * half, half), half)
    part_at = pl.ds(pl.multiple_of(c * half + x * part, part), part)
    in_half = pl.ds(pl.multiple_of(x * part, part), part)
    flight = {}
    sent = []

    def await_all(r, stage):
        for copy in flight[r, stage]:
            copy.wait_recv()
        sent.extend(flight[r, stage])

    def stage_run(r, stage):
        out = []
        if stage == 0:
            grams(r)
            for d in range(1, nc):
                to = peer(c, d, nc)
                at = pl.ds(pl.multiple_of(to * half, half), half)
                out.append(remote(gf.at[r, :, at, :], r1.at[r, d - 1], c_s.at[r, d], c_r.at[r, d], "blk", to))
        elif stage == 1:
            await_all(r, 0)
            total = gf[r, :, half_at, :]
            for d in range(1, nc):
                total = total + r1[r, d - 1]
            b2[r] = total.astype(BF16)
            gf[r, :, half_at, :] = total
            for d in range(1, nx):
                to = peer(x, d, nx)
                at = pl.ds(pl.multiple_of(to * part, part), part)
                out.append(remote(b2.at[r, :, at, :], r2.at[r, d - 1], x_s.at[r, d], x_r.at[r, d], "space", to))
        elif stage == 2:
            await_all(r, 1)
            total = gf[r, :, part_at, :]
            for d in range(1, nx):
                total = total + r2[r, d - 1].astype(F32)
            b3[r] = total.astype(BF16)
            gf[r, :, part_at, :] = total
            for d in range(nz - 1, 0, -1):
                to = peer(z, d, nz)
                out.append(remote(b3.at[r, to], r3.at[r, d - 1], z_s.at[r, d], z_r.at[r, d], "freq", to))
        elif stage == 3:
            await_all(r, 2)
            total = gf[r, z, part_at, :]
            for d in range(1, nz):
                total = total + r3[r, d - 1].astype(F32)
            gfull[r, z, part_at, :] = (total * gram_scale).astype(BF16)
            block = gfull.at[r, z, part_at, :]
            for d in range(nz - 1, 0, -1):
                to = peer(z, d, nz)
                out.append(remote(block, block, gz_s.at[r, d], gz_r.at[r, d], "freq", to))
        elif stage == 4:
            await_all(r, 3)
            block = gfull.at[r, :, part_at, :]
            for d in range(1, nx):
                out.append(remote(block, block, gx_s.at[r, d], gx_r.at[r, d], "space", peer(x, d, nx)))
        elif stage == 5:
            await_all(r, 4)
            block = gfull.at[r, :, half_at, :]
            for d in range(1, nc):
                out.append(remote(block, block, gc_s.at[r, d], gc_r.at[r, d], "blk", peer(c, d, nc)))
        else:
            await_all(r, 5)
            gram_ref[r] = gfull[r, z].astype(F32)
        flight[r, stage] = out

    for tick in range(7 + rounds - 1):
        for r in range(rounds):
            if 0 <= tick - r < 7:
                stage_run(r, tick - r)

    def modes(zk):
        def one(i, carry):
            total = None
            at = pl.multiple_of(i * 2 * nb, 2 * nb)
            for r in range(rounds):
                p = partners_ref[r, zk]
                re = gfull[r, zk, pl.ds(at, nb), :]
                im = gfull[r, zk, pl.ds(at + nb, nb), :]
                left = jnp.concatenate([jnp.concatenate([re, -im], axis=1),
                                        jnp.concatenate([im, re], axis=1)], axis=0)
                term = jnp.dot(left, targets(zk, p, i), preferred_element_type=F32)
                total = term if total is None else total + term
            mo[zk, pl.ds(at, 2 * nb), :] = (total * mode_scale).astype(BF16)
            return carry

        lax.fori_loop(0, per, one, 0)

    outgoing = []
    for d in range(nz - 1, 0, -1):
        to = peer(z, d, nz)
        modes(to)
        outgoing.append(remote(mo.at[to], out_ref.at[z], out_s.at[d], out_r.at[d], "freq", to))
    modes(z)
    keep = pltpu.make_async_copy(mo.at[z], out_ref.at[z], own_sem)
    keep.start()
    keep.wait()
    for copy in outgoing:
        copy.wait_recv()
    for copy in incoming + sent + outgoing:
        copy.wait_send()


def body(sizes, realizations, weights, partners, block_count):
    nz, nx, nc = sizes
    per, nb, _, points = realizations.shape
    rounds = partners.shape[0]
    pts = points // nz
    keeper = (jnp.arange(nb, dtype=jnp.int32) < block_count[0]).astype(BF16)
    fields = realizations * keeper[None, :, None, None]
    fields = fields.reshape(per, nb, 2, nz, pts).transpose(3, 2, 0, 1, 4)
    width = per * nb
    rows = 2 * per * nb
    half = rows // nc
    part = half // nx
    freqs = nz * per
    dims = (nz, nx, nc, rounds, per, nb, pts,
            1.0 / math.sqrt(points * nx * nc), 1.0 / math.sqrt(rounds * per * nb))
    dma = pltpu.SemaphoreType.DMA
    vmem = pl.BlockSpec(memory_space=pltpu.VMEM)
    modes, grams = pl.pallas_call(
        functools.partial(kernel, dims),
        out_shape=(jax.ShapeDtypeStruct((nz, rows, pts), BF16),
                   jax.ShapeDtypeStruct((rounds, rows, width), F32)),
        in_specs=[pl.BlockSpec(memory_space=pltpu.SMEM), vmem, vmem],
        out_specs=(vmem, vmem),
        scratch_shapes=[
            pltpu.VMEM((2, freqs, nb, pts), BF16),
            pltpu.VMEM((2, freqs, nb, pts), F32),
            pltpu.VMEM((2, per, nb, pts), F32),
            pltpu.VMEM((2 * width, pts), BF16),
            pltpu.VMEM((rounds, nz, rows, width), F32),
            pltpu.VMEM((rounds, nc - 1, nz, half, width), F32),
            pltpu.VMEM((rounds, nz, half, width), BF16),
            pltpu.VMEM((rounds, nx - 1, nz, part, width), BF16),
            pltpu.VMEM((rounds, nz, part, width), BF16),
            pltpu.VMEM((rounds, nz - 1, part, width), BF16),
            pltpu.VMEM((rounds, nz, rows, width), BF16),
            pltpu.VMEM((nz, rows, pts), BF16),
            dma,
            dma((nz,)), dma((nz,)),
            dma((rounds, nc)), dma((rounds, nc)),
            dma((rounds, nx)), dma((rounds, nx)),
            dma((rounds, nz)), dma((rounds, nz)),
            dma((rounds, nz)), dma((rounds, nz)),
            dma((rounds, nx)), dma((rounds, nx)),
            dma((rounds, nc)), dma((rounds, nc)),
            dma((nz,)), dma((nz,)),
        ],
        compiler_params=pltpu.CompilerParams(
            collective_id=0, has_side_effects=True, vmem_limit_bytes=56 * 1024 * 1024),
    )(partners, fields, weights.reshape(nz, pts))
    modes = modes.reshape(nz, per, 2, nb, pts).transpose(1, 3, 2, 0, 4).reshape(per, nb, 2, points)
    grams = grams.reshape(rounds, per, 2, nb, per, nb).transpose(0, 1, 4, 2, 3, 5)
    return (modes, grams)


def solution(mesh):
    placed = (
        P("freq", "groups", None, ("space", "blk")),
        P(("groups", "space", "blk")),
        P(),
        P("groups"),
    )
    return jax.shard_map(
        functools.partial(body, tuple(mesh.shape[a] for a in AXES)),
        mesh=mesh,
        in_specs=placed,
        out_specs=(
            P("freq", "groups", None, ("space", "blk")),
            P("groups", "freq", None, None, None, None),
        ),
        check_vma=False,
    )
```

time: 217 us -> 103 us (0.47)
  waiting for transfers between devices: 121 us -> 0 us
  Pallas kernels: 0 us -> 90.2 us
  local copies, waits for them, and re-layouts: 45.3 us -> 8.67 us
  matrix products: 25.9 us -> 0 us
  between operations: 17 us -> 1.32 us
  other arithmetic: 7.77 us -> 2.19 us
    pallas_call x0 -> x1, Pallas kernels: none -> 90.2 us  [body(): pl.pallas_call(functools.partial(kernel, dims), out_shape=(jax.ShapeDtype...]
    all_gather x1 -> x0, waiting for transfers between devices: 79.3 us -> none  [body(): gathered = lax.all_gather(fields, 'freq', axis=0, tiled=True)]
    psum x1 -> x0, waiting for transfers between devices: 41.5 us -> none  [body(): grams = lax.psum(partial_value, ('space', 'blk')) * gram_scale]
    gather x9 -> x0, local copies, waits for them, and re-layouts: 31.9 us -> none  [the longest x6 23.5 us: body(): targets = gathered[target_idx]]
    dot_general x24 -> x0, matrix products: 25.9 us -> none  [the longest x3 5.19 us: body(): jnp.einsum('ijas,ijbs->ijab', prod_real, target_imag, preferred_element_t...]
    unnamed x48 -> x2, local copies, waits for them, and re-layouts: 7.75 us -> 0.01 us
    reshape x0 -> x6, local copies, waits for them, and re-layouts: none -> 6.58 us  [the longest x2 2.06 us: body(): grams.reshape(rounds, per, 2, nb, per, nb).transpose(0, 1, 4, 2, 3, 5)]
    mul x4 -> x0, local copies, waits for them, and re-layouts: 4.69 us -> none  [body(): first_real * second[:, :, :, 0] - first_imag * second[:, :, :, 1]]
  transfers between devices with their start and end apart: 2 -> 0, of which waited for: 2 -> 0; matrix products, arithmetic and copies ran while one was open for 1% -> 0% of each run, Pallas kernels for 0% -> 0%
where the time goes in v1:
time: 103 us; the launch traced here: 102 us
  Pallas kernels  90.2 us (88%)
  local copies, waits for them, and re-layouts  8.67 us (8%)
  other arithmetic  2.19 us (2%)
  between operations  1.32 us (1%)
    pallas_call x1, Pallas kernels, body(): pl.pallas_call(functools.partial(kernel, dims), out_shape=(jax.ShapeDtype...  90.2 us
    mul x1, other arithmetic, body(): fields = realizations * keeper[None, :, None, None]  2.18 us
    transpose x1, local copies, waits for them, and re-layouts, body(): modes.reshape(nz, per, 2, nb, pts).transpose(1, 3, 2, 0, 4)  2.09 us

profile of v1, /device:TPU:0, one launch (start us, length us, event | category | flops | bytes accessed | tf_op | source)
XLA Modules:
  0.0 102.4 jit_solution(10910928697997556886)
XLA Ops:
  1.3 1.3 %reshape.25.w_ref = f32[4,512]{1,0:T(4,128)} reshape(f32[2048]{0:T(1024)} %param.5) | data formatting | bytes 16384 | tf_op jit(solution)/shard_map/reshape | solution.py:255
  2.6 2.2 %broadcast_multiply_fusion = bf16[4,32,2,2048]{3,2,1,0:T(2,128)(2,1)S(1)} fusion(bf16[4,32,2,2048]{3,2,1,0:T(2,128)(2,1)} %param.4, bf16[32]{0:T(256)(128)(2,1)S(1)} %compare_convert_fusion), kind=kLoop, calls=%fused_computation.2 | loop fusion | flops 524288 | bytes 2097216 | tf_op jit(solution)/shard_map/mul | solution.py:213
  4.8 0.7 reshape.29
  5.5 1.3 %copy.17 = bf16[4,32,2,4,512]{4,1,0,2,3:T(8,128)(2,1)} copy(bf16[4,32,2,4,512]{4,3,2,1,0:T(4,128)(2,1)S(1)} %reshape.29) | data formatting | bytes 2097152 | tf_op jit(solution)/shard_map/reshape | solution.py:214
  6.8 90.2 %shard_map.59 = (bf16[4,256,512]{2,1,0:T(8,128)(2,1)}, f32[3,256,128]{2,1,0:T(8,128)}) custom-call(s32[3,4]{1,0:T(4,128)} %partners_ref.1, bf16[4,2,4,32,512]{4,3,2,1,0:T(8,128)(2,1)} %bitcast.11, f32[4,512]{1,0:T(4,128)} %reshape.25.w_ref), custom_call_target="tpu_custom_call" | custom-call | tf_op jit(solution)/shard_map/pallas_call | solution.py:224
  97.0 0.0 copy-start
  97.0 2.1 %copy.10 = bf16[4,32,2,4,512]{4,3,2,1,0:T(4,128)(2,1)S(1)} copy(bf16[4,32,2,4,512]{4,1,2,0,3:T(8,128)(2,1)} %bitcast.13) | data formatting | bytes 2097152 | tf_op jit(solution)/shard_map/transpose | solution.py:256
  99.1 1.2 %reshape.27 = bf16[4,32,2,2048]{3,2,1,0:T(2,128)(2,1)} reshape(bf16[4,32,2,4,512]{4,3,2,1,0:T(4,128)(2,1)S(1)} %copy.10) | data formatting | bytes 2097152 | tf_op jit(solution)/shard_map/reshape | solution.py:256
  100.3 0.0 copy-done
  100.3 0.7 reshape.28
  101.0 1.4 %copy.16 = f32[3,4,2,32,4,32]{5,3,2,4,1,0:T(8,128)} copy(f32[3,4,2,32,4,32]{5,4,3,2,1,0:T(4,128)S(1)} %reshape.28) | data formatting | bytes 786432 | tf_op jit(solution)/shard_map/reshape | solution.py:257
  (1 shorter events, 0.0 us)
Async XLA Ops:
  97.0 3.3 %copy-start = (f32[3,256,128]{2,1,0:T(8,128)S(1)}, f32[3,256,128]{2,1,0:T(8,128)}, u32[]{:S(2)}) copy-start(f32[3,256,128]{2,1,0:T(8,128)} %get-tuple-element.5) | copy-start | bytes 1179652

commit v2 on v1

v2 whole, which is shorter than its diff:
```python
import functools
import math

import jax
import jax.numpy as jnp
from jax import lax
from jax.experimental import pallas as pl
from jax.experimental.pallas import tpu as pltpu
from jax.sharding import PartitionSpec as P

MESH = pl.DeviceIdType.MESH
F32 = jnp.float32
BF16 = jnp.bfloat16
AXES = ("freq", "space", "blk")


def kernel(dims, partners_ref, count_ref, x_ref, w_ref, out_ref, gram_ref,
           q, qf, wq, prod, gf, r1, b2, r2, b3, r3, gfull, mo,
           own_sem, in_s, in_r, c_s, c_r, x_s, x_r, z_s, z_r,
           gz_s, gz_r, gx_s, gx_r, gc_s, gc_r, out_s, out_r):
    nz, nx, nc, rounds, per, nb, pts, halves, chunks, gram_scale, mode_scale = dims
    width = per * nb
    each = per // chunks
    rows = each * 2 * nb
    half = rows // nc
    part = half // nx
    freqs = nz * per
    z = lax.axis_index("freq")
    x = lax.axis_index("space")
    c = lax.axis_index("blk")

    def peer(me, d, n):
        return lax.rem(me + d, n)

    barrier = pltpu.get_barrier_semaphore()
    for name, me, n in (("freq", z, nz), ("space", x, nx), ("blk", c, nc)):
        for d in range(1, n):
            pl.semaphore_signal(barrier, inc=1, device_id={name: peer(me, d, n)}, device_id_type=MESH)
    pl.semaphore_wait(barrier, nz + nx + nc - 3)

    def remote(src, dst, send, recv, name, to):
        copy = pltpu.make_async_remote_copy(
            src_ref=src, dst_ref=dst, send_sem=send, recv_sem=recv,
            device_id={name: to}, device_id_type=MESH)
        copy.start()
        return copy

    incoming, kept = [], []
    mine = pl.ds(z * per, per)
    for h in range(halves):
        arriving = []
        for d in range(nz - 1, 0, -1):
            to = peer(z, d, nz)
            arriving.append(remote(x_ref.at[to * halves + h], q[h].at[:, mine],
                                   in_s.at[h, d], in_r.at[h, d], "freq", to))
        own = pltpu.make_async_copy(x_ref.at[z * halves + h], q[h].at[:, mine], own_sem.at[h])
        own.start()
        incoming.append(arriving)
        kept.append(own)

    lane_j = lax.broadcasted_iota(jnp.int32, (nb, width), 1) // nb

    def arrive(h):
        kept[h].wait()
        for copy in incoming[h]:
            copy.wait_recv()
        weights = w_ref[:, pl.ds(pl.multiple_of((z * halves + h) * pts, pts), pts)]

        def widen(f, carry):
            for e in range(2):
                value = q[h][e, f].astype(F32)
                qf[e, f] = value
                wq[e, f] = value * weights
            return carry

        lax.fori_loop(0, freqs, widen, 0)

    def targets(h, g, p, i):
        at = [lax.rem((g + p) * per + i + j, freqs) for j in range(per)]
        return jnp.concatenate([q[h][e, t] for e in range(2) for t in at], axis=0)

    def grams(h, ch):
        def one(step, carry):
            r = step // nz
            g = step % nz
            p = partners_ref[r, g]
            for ii in range(each):
                i = ch * each + ii
                first_re = wq[0, g * per + i]
                first_im = wq[1, g * per + i]
                for j in range(per):
                    second_re = qf[0, p * per + j]
                    second_im = qf[1, p * per + j]
                    prod[pl.ds(j * nb, nb), :] = (first_re * second_re - first_im * second_im).astype(BF16)
                    prod[pl.ds(width + j * nb, nb), :] = (first_re * second_im + first_im * second_re).astype(BF16)
                full = lax.dot_general(prod[...], targets(h, g, p, i), (((1,), (1,)), ((), ())),
                                       preferred_element_type=F32)
                g_re = full[:width, :width] + full[width:, width:]
                g_im = full[:width, width:] - full[width:, :width]
                re, im = g_re[:nb], g_im[:nb]
                for j in range(1, per):
                    keep = lane_j == j
                    re = jnp.where(keep, g_re[j * nb:(j + 1) * nb], re)
                    im = jnp.where(keep, g_im[j * nb:(j + 1) * nb], im)
                both = jnp.concatenate([re, im], axis=0)
                at = pl.ds(ii * 2 * nb, 2 * nb)
                if h > 0:
                    both = both + gf[ch, r, g, at, :]
                gf[ch, r, g, at, :] = both
            return carry

        lax.fori_loop(0, rounds * nz, one, 0)

    half_at = pl.ds(pl.multiple_of(c * half, half), half)
    part_at = pl.ds(pl.multiple_of(c * half + x * part, part), part)
    flight = {}
    sent = []

    def await_all(ch, stage):
        for copy in flight[ch, stage]:
            copy.wait_recv()
        sent.extend(flight[ch, stage])

    def modes(ch, zk):
        for ii in range(each):
            i = ch * each + ii
            at = ii * 2 * nb
            totals = [None] * halves
            for r in range(rounds):
                p = partners_ref[r, zk]
                re = gfull[ch, r, zk, pl.ds(at, nb), :]
                im = gfull[ch, r, zk, pl.ds(at + nb, nb), :]
                left = jnp.concatenate([jnp.concatenate([re, -im], axis=1),
                                        jnp.concatenate([im, re], axis=1)], axis=0)
                for h in range(halves):
                    term = jnp.dot(left, targets(h, zk, p, i), preferred_element_type=F32)
                    totals[h] = term if totals[h] is None else totals[h] + term
            for h in range(halves):
                mo[zk * halves + h, pl.ds(ch * rows + at, 2 * nb), :] = (totals[h] * mode_scale).astype(BF16)

    def stage_run(ch, stage):
        out = []
        if stage == 0:
            grams(halves - 1, ch)
            for d in range(1, nc):
                to = peer(c, d, nc)
                at = pl.ds(pl.multiple_of(to * half, half), half)
                out.append(remote(gf.at[ch, :, :, at, :], r1.at[ch, d - 1], c_s.at[ch, d], c_r.at[ch, d], "blk", to))
        elif stage == 1:
            await_all(ch, 0)
            total = gf[ch, :, :, half_at, :]
            for d in range(1, nc):
                total = total + r1[ch, d - 1]
            b2[ch] = total.astype(BF16)
            gf[ch, :, :, half_at, :] = total
            for d in range(1, nx):
                to = peer(x, d, nx)
                at = pl.ds(pl.multiple_of(to * part, part), part)
                out.append(remote(b2.at[ch, :, :, at, :], r2.at[ch, d - 1], x_s.at[ch, d], x_r.at[ch, d], "space", to))
        elif stage == 2:
            await_all(ch, 1)
            total = gf[ch, :, :, part_at, :]
            for d in range(1, nx):
                total = total + r2[ch, d - 1].astype(F32)
            b3[ch] = total.astype(BF16)
            gf[ch, :, :, part_at, :] = total
            for d in range(nz - 1, 0, -1):
                to = peer(z, d, nz)
                out.append(remote(b3.at[ch, :, to], r3.at[ch, d - 1], z_s.at[ch, d], z_r.at[ch, d], "freq", to))
        elif stage == 3:
            await_all(ch, 2)
            total = gf[ch, :, z, part_at, :]
            for d in range(1, nz):
                total = total + r3[ch, d - 1].astype(F32)
            row = lax.broadcasted_iota(jnp.int32, (part, width), 0) + (c * half + x * part)
            lane = lax.broadcasted_iota(jnp.int32, (part, width), 1)
            last = jnp.maximum(lax.rem(row, nb), lax.rem(lane, nb))
            total = jnp.where((last < count_ref[0])[None], total * gram_scale, 0.0)
            gfull[ch, :, z, part_at, :] = total.astype(BF16)
            block = gfull.at[ch, :, z, part_at, :]
            for d in range(nz - 1, 0, -1):
                to = peer(z, d, nz)
                out.append(remote(block, block, gz_s.at[ch, d], gz_r.at[ch, d], "freq", to))
        elif stage == 4:
            await_all(ch, 3)
            block = gfull.at[ch, :, :, part_at, :]
            for d in range(1, nx):
                out.append(remote(block, block, gx_s.at[ch, d], gx_r.at[ch, d], "space", peer(x, d, nx)))
        elif stage == 5:
            await_all(ch, 4)
            block = gfull.at[ch, :, :, half_at, :]
            for d in range(1, nc):
                out.append(remote(block, block, gc_s.at[ch, d], gc_r.at[ch, d], "blk", peer(c, d, nc)))
        else:
            await_all(ch, 5)
            at = pl.ds(ch * rows, rows)
            for d in range(nz - 1, 0, -1):
                to = peer(z, d, nz)
                modes(ch, to)
                out.append(remote(mo.at[pl.ds(to * halves, halves), at, :],
                                  out_ref.at[pl.ds(z * halves, halves), at, :],
                                  out_s.at[ch, d], out_r.at[ch, d], "freq", to))
            modes(ch, z)
        flight[ch, stage] = out

    for h in range(halves):
        arrive(h)
        if h < halves - 1:
            for ch in range(chunks):
                grams(h, ch)
    for tick in range(7 + chunks - 1):
        for ch in range(chunks - 1, -1, -1):
            if 0 <= tick - ch < 7:
                stage_run(ch, tick - ch)

    own = pltpu.make_async_copy(mo.at[pl.ds(z * halves, halves)], out_ref.at[pl.ds(z * halves, halves)], own_sem.at[0])
    own.start()
    for ch in range(chunks):
        for r in range(rounds):
            for ii in range(each):
                for e in range(2):
                    value = gfull[ch, r, z, pl.ds((ii * 2 + e) * nb, nb), :].astype(F32)
                    for j in range(per):
                        gram_ref[r, ch * each + ii, j, e] = value[:, j * nb:(j + 1) * nb]
    own.wait()
    for ch in range(chunks):
        await_all(ch, 6)
    for copy in sum(incoming, []) + sent:
        copy.wait_send()


def body(sizes, realizations, weights, partners, block_count):
    nz, nx, nc = sizes
    per, nb, _, points = realizations.shape
    rounds = partners.shape[0]
    halves = 2 if points % (nz * 256) == 0 else 1
    pts = points // (nz * halves)
    chunks = max(1, min(per, per * 2 * nb // (nc * nx * 16)))
    fields = realizations.reshape(per, nb, 2, nz * halves, pts).transpose(3, 2, 0, 1, 4)
    width = per * nb
    rows = 2 * width // chunks
    half = rows // nc
    part = half // nx
    freqs = nz * per
    dims = (nz, nx, nc, rounds, per, nb, pts, halves, chunks,
            1.0 / math.sqrt(points * nx * nc), 1.0 / math.sqrt(rounds * per * nb))
    dma = pltpu.SemaphoreType.DMA
    vmem = pl.BlockSpec(memory_space=pltpu.VMEM)
    smem = pl.BlockSpec(memory_space=pltpu.SMEM)
    modes, grams = pl.pallas_call(
        functools.partial(kernel, dims),
        out_shape=(jax.ShapeDtypeStruct((nz * halves, 2 * width, pts), BF16),
                   jax.ShapeDtypeStruct((rounds, per, per, 2, nb, nb), F32)),
        in_specs=[smem, smem, vmem, vmem],
        out_specs=(vmem, vmem),
        scratch_shapes=[
            tuple(pltpu.VMEM((2, freqs, nb, pts), BF16) for _ in range(halves)),
            pltpu.VMEM((2, freqs, nb, pts), F32),
            pltpu.VMEM((2, freqs, nb, pts), F32),
            pltpu.VMEM((2 * width, pts), BF16),
            pltpu.VMEM((chunks, rounds, nz, rows, width), F32),
            pltpu.VMEM((chunks, nc - 1, rounds, nz, half, width), F32),
            pltpu.VMEM((chunks, rounds, nz, half, width), BF16),
            pltpu.VMEM((chunks, nx - 1, rounds, nz, part, width), BF16),
            pltpu.VMEM((chunks, rounds, nz, part, width), BF16),
            pltpu.VMEM((chunks, nz - 1, rounds, part, width), BF16),
            pltpu.VMEM((chunks, rounds, nz, rows, width), BF16),
            pltpu.VMEM((nz * halves, 2 * width, pts), BF16),
            dma((halves,)),
            dma((halves, nz)), dma((halves, nz)),
            dma((chunks, nc)), dma((chunks, nc)),
            dma((chunks, nx)), dma((chunks, nx)),
            dma((chunks, nz)), dma((chunks, nz)),
            dma((chunks, nz)), dma((chunks, nz)),
            dma((chunks, nx)), dma((chunks, nx)),
            dma((chunks, nc)), dma((chunks, nc)),
            dma((chunks, nz)), dma((chunks, nz)),
        ],
        compiler_params=pltpu.CompilerParams(
            collective_id=0, has_side_effects=True, vmem_limit_bytes=56 * 1024 * 1024),
    )(partners, block_count, fields, weights.reshape(1, points))
    modes = modes.reshape(nz * halves, per, 2, nb, pts).transpose(1, 3, 2, 0, 4).reshape(per, nb, 2, points)
    return (modes, grams)


def solution(mesh):
    placed = (
        P("freq", "groups", None, ("space", "blk")),
        P(("groups", "space", "blk")),
        P(),
        P("groups"),
    )
    return jax.shard_map(
        functools.partial(body, tuple(mesh.shape[a] for a in AXES)),
        mesh=mesh,
        in_specs=placed,
        out_specs=(
            P("freq", "groups", None, ("space", "blk")),
            P("groups", "freq", None, None, None, None),
        ),
        check_vma=False,
    )
```

time: 103 us -> 94.9 us (0.921)
  Pallas kernels: 90.2 us -> 86.1 us
  other arithmetic: 2.19 us -> 0 us
  local copies, waits for them, and re-layouts: 8.67 us -> 7.24 us
    pallas_call x1, Pallas kernels: 90.2 us -> 86.1 us  [body(): pl.pallas_call(functools.partial(kernel, dims), out_shape=(jax.ShapeDtype...]
    reshape x6 -> x3, local copies, waits for them, and re-layouts: 6.58 us -> 4.16 us  [the longest x2 3.05 us: body(): realizations.reshape(per, nb, 2, nz * halves, pts).transpose(3, 2, 0, 1, 4)]
    mul x1 -> x0, other arithmetic: 2.18 us -> none  [body(): fields = realizations * keeper[None, :, None, None]]
    unnamed x2 -> x3, local copies, waits for them, and re-layouts: 0.01 us -> 1.15 us
where the time goes in v2:
time: 94.9 us; the launch traced here: 94.7 us
  Pallas kernels  86.1 us (91%)
  local copies, waits for them, and re-layouts  7.24 us (8%)
  between operations  1.3 us (1%)
    pallas_call x1, Pallas kernels, body(): pl.pallas_call(functools.partial(kernel, dims), out_shape=(jax.ShapeDtype...  86.1 us
    reshape x2, local copies, waits for them, and re-layouts, body(): realizations.reshape(per, nb, 2, nz * halves, pts).transpose(3, 2, 0, 1, 4)  3.05 us
    transpose x1, local copies, waits for them, and re-layouts, body(): modes.reshape(nz * halves, per, 2, nb, pts).transpose(1, 3, 2, 0, 4)  1.93 us

profile of v2, /device:TPU:0, one launch (start us, length us, event | category | flops | bytes accessed | tf_op | source)
XLA Modules:
  0.0 94.7 jit_solution(2199279643007270375)
XLA Ops:
  1.3 1.7 %reshape.20 = bf16[4,32,2,8,256]{4,3,2,1,0:T(8,128)(2,1)S(1)} reshape(bf16[4,32,2,2048]{3,2,1,0:T(2,128)(2,1)} %param.4) | data formatting | bytes 2097152 | tf_op jit(solution)/shard_map/reshape | solution.py:239
  3.0 1.3 %copy.13 = bf16[4,32,2,8,256]{4,1,0,2,3:T(8,128)(2,1)} copy(bf16[4,32,2,8,256]{4,3,2,1,0:T(8,128)(2,1)S(1)} %reshape.20) | data formatting | bytes 2097152 | tf_op jit(solution)/shard_map/reshape | solution.py:239
  4.3 86.1 %shard_map.59 = (bf16[8,256,256]{2,1,0:T(8,128)(2,1)}, f32[3,4,4,2,32,32]{5,4,3,2,1,0:T(8,128)}) custom-call(s32[3,4]{1,0:T(4,128)} %partners_ref.1, s32[1]{0:T(128)S(6)} %copy.15.count_ref, bf16[8,2,4,32,256]{4,3,2,1,0:T(8,128)(2,1)} %bitcast.9, f32[1,2048]{1,0:T(1,128)} %bitcast.11), custom_call_target="tpu_custom_call" | custom-call | tf_op jit(solution)/shard_map/pallas_call | solution.py:250
  90.5 0.0 copy-start
  90.5 1.9 %copy.9 = bf16[4,32,2,8,256]{4,3,2,1,0:T(8,128)(2,1)S(1)} copy(bf16[4,32,2,8,256]{4,1,2,0,3:T(8,128)(2,1)} %bitcast.10) | data formatting | bytes 2097152 | tf_op jit(solution)/shard_map/transpose | solution.py:282
  92.4 1.1 %reshape.19 = bf16[4,32,2,2048]{3,2,1,0:T(2,128)(2,1)} reshape(bf16[4,32,2,8,256]{4,3,2,1,0:T(8,128)(2,1)S(1)} %copy.9) | data formatting | bytes 2097152 | tf_op jit(solution)/shard_map/reshape | solution.py:282
  93.5 0.0 copy-done
  93.5 1.1 %copy.16 = f32[3,4,4,2,32,32]{5,4,3,2,1,0:T(8,128)} copy(f32[3,4,4,2,32,32]{5,4,3,2,1,0:T(8,128)S(1)} %copy-done) | data formatting | bytes 786432
Async XLA Ops:
  90.5 3.1 %copy-start = (f32[3,4,4,2,32,32]{5,4,3,2,1,0:T(8,128)S(1)}, f32[3,4,4,2,32,32]{5,4,3,2,1,0:T(8,128)}, u32[]{:S(2)}) copy-start(f32[3,4,4,2,32,32]{5,4,3,2,1,0:T(8,128)} %get-tuple-element.9) | copy-start | bytes 1179652

commit v3 on v2

--- a/solution.py
+++ b/solution.py
@@ -15,7 +15,7 @@
 
 
 def kernel(dims, partners_ref, count_ref, x_ref, w_ref, out_ref, gram_ref,
-           q, qf, wq, prod, gf, r1, b2, r2, b3, r3, gfull, mo,
+           q, qf, wq, gf, r1, b2, r2, b3, r3, gfull, mo,
            own_sem, in_s, in_r, c_s, c_r, x_s, x_r, z_s, z_r,
            gz_s, gz_r, gx_s, gx_r, gc_s, gc_r, out_s, out_r):
     nz, nx, nc, rounds, per, nb, pts, halves, chunks, gram_scale, mode_scale = dims
@@ -80,36 +80,36 @@
         return jnp.concatenate([q[h][e, t] for e in range(2) for t in at], axis=0)
 
     def grams(h, ch):
-        def one(step, carry):
-            r = step // nz
-            g = step % nz
-            p = partners_ref[r, g]
-            for ii in range(each):
-                i = ch * each + ii
-                first_re = wq[0, g * per + i]
-                first_im = wq[1, g * per + i]
-                for j in range(per):
-                    second_re = qf[0, p * per + j]
-                    second_im = qf[1, p * per + j]
-                    prod[pl.ds(j * nb, nb), :] = (first_re * second_re - first_im * second_im).astype(BF16)
-                    prod[pl.ds(width + j * nb, nb), :] = (first_re * second_im + first_im * second_re).astype(BF16)
-                full = lax.dot_general(prod[...], targets(h, g, p, i), (((1,), (1,)), ((), ())),
-                                       preferred_element_type=F32)
-                g_re = full[:width, :width] + full[width:, width:]
-                g_im = full[:width, width:] - full[width:, :width]
-                re, im = g_re[:nb], g_im[:nb]
-                for j in range(1, per):
-                    keep = lane_j == j
-                    re = jnp.where(keep, g_re[j * nb:(j + 1) * nb], re)
-                    im = jnp.where(keep, g_im[j * nb:(j + 1) * nb], im)
-                both = jnp.concatenate([re, im], axis=0)
-                at = pl.ds(ii * 2 * nb, 2 * nb)
-                if h > 0:
-                    both = both + gf[ch, r, g, at, :]
-                gf[ch, r, g, at, :] = both
+        def one(g, carry):
+            for r in range(rounds):
+                p = partners_ref[r, g]
+                for ii in range(each):
+                    i = ch * each + ii
+                    first_re = wq[0, g * per + i]
+                    first_im = wq[1, g * per + i]
+                    reals, imags = [], []
+                    for j in range(per):
+                        second_re = qf[0, p * per + j]
+                        second_im = qf[1, p * per + j]
+                        reals.append((first_re * second_re - first_im * second_im).astype(BF16))
+                        imags.append((first_re * second_im + first_im * second_re).astype(BF16))
+                    full = lax.dot_general(jnp.concatenate(reals + imags, axis=0), targets(h, g, p, i),
+                                           (((1,), (1,)), ((), ())), preferred_element_type=F32)
+                    g_re = full[:width, :width] + full[width:, width:]
+                    g_im = full[:width, width:] - full[width:, :width]
+                    re, im = g_re[:nb], g_im[:nb]
+                    for j in range(1, per):
+                        keep = lane_j == j
+                        re = jnp.where(keep, g_re[j * nb:(j + 1) * nb], re)
+                        im = jnp.where(keep, g_im[j * nb:(j + 1) * nb], im)
+                    both = jnp.concatenate([re, im], axis=0)
+                    at = pl.ds(ii * 2 * nb, 2 * nb)
+                    if h > 0:
+                        both = both + gf[ch, r, g, at, :]
+                    gf[ch, r, g, at, :] = both
             return carry
 
-        lax.fori_loop(0, rounds * nz, one, 0)
+        lax.fori_loop(0, nz, one, 0)
 
     half_at = pl.ds(pl.multiple_of(c * half, half), half)
     part_at = pl.ds(pl.multiple_of(c * half + x * part, part), part)
@@ -257,7 +257,6 @@
             tuple(pltpu.VMEM((2, freqs, nb, pts), BF16) for _ in range(halves)),
             pltpu.VMEM((2, freqs, nb, pts), F32),
             pltpu.VMEM((2, freqs, nb, pts), F32),
-            pltpu.VMEM((2 * width, pts), BF16),
             pltpu.VMEM((chunks, rounds, nz, rows, width), F32),
             pltpu.VMEM((chunks, nc - 1, rounds, nz, half, width), F32),
             pltpu.VMEM((chunks, rounds, nz, half, width), BF16),

time: 94.9 us -> 85.3 us (0.90)
  Pallas kernels: 86.1 us -> 76.6 us
    pallas_call x1, Pallas kernels: 86.1 us -> 76.6 us  [body(): pl.pallas_call(functools.partial(kernel, dims), out_shape=(jax.ShapeDtype...]
where the time goes in v3:
time: 85.3 us; the launch traced here: 85.1 us
  Pallas kernels  76.6 us (90%)
  local copies, waits for them, and re-layouts  7.24 us (8%)
  between operations  1.3 us (2%)
    pallas_call x1, Pallas kernels, body(): pl.pallas_call(functools.partial(kernel, dims), out_shape=(jax.ShapeDtype...  76.6 us
    reshape x2, local copies, waits for them, and re-layouts, body(): realizations.reshape(per, nb, 2, nz * halves, pts).transpose(3, 2, 0, 1, 4)  3.05 us
    transpose x1, local copies, waits for them, and re-layouts, body(): modes.reshape(nz * halves, per, 2, nb, pts).transpose(1, 3, 2, 0, 4)  1.93 us

profile of v3, /device:TPU:0, one launch (start us, length us, event | category | flops | bytes accessed | tf_op | source)
XLA Modules:
  0.0 85.1 jit_solution(15660557160602325600)
XLA Ops:
  1.3 1.7 %reshape.20 = bf16[4,32,2,8,256]{4,3,2,1,0:T(8,128)(2,1)S(1)} reshape(bf16[4,32,2,2048]{3,2,1,0:T(2,128)(2,1)} %param.4) | data formatting | bytes 2097152 | tf_op jit(solution)/shard_map/reshape | solution.py:239
  3.0 1.3 %copy.13 = bf16[4,32,2,8,256]{4,1,0,2,3:T(8,128)(2,1)} copy(bf16[4,32,2,8,256]{4,3,2,1,0:T(8,128)(2,1)S(1)} %reshape.20) | data formatting | bytes 2097152 | tf_op jit(solution)/shard_map/reshape | solution.py:239
  4.3 76.6 %shard_map.59 = (bf16[8,256,256]{2,1,0:T(8,128)(2,1)}, f32[3,4,4,2,32,32]{5,4,3,2,1,0:T(8,128)}) custom-call(s32[3,4]{1,0:T(4,128)} %partners_ref.1, s32[1]{0:T(128)S(6)} %copy.15.count_ref, bf16[8,2,4,32,256]{4,3,2,1,0:T(8,128)(2,1)} %bitcast.9, f32[1,2048]{1,0:T(1,128)} %bitcast.11), custom_call_target="tpu_custom_call" | custom-call | tf_op jit(solution)/shard_map/pallas_call | solution.py:250
  80.9 0.0 copy-start
  80.9 1.9 %copy.9 = bf16[4,32,2,8,256]{4,3,2,1,0:T(8,128)(2,1)S(1)} copy(bf16[4,32,2,8,256]{4,1,2,0,3:T(8,128)(2,1)} %bitcast.10) | data formatting | bytes 2097152 | tf_op jit(solution)/shard_map/transpose | solution.py:281
  82.9 1.1 %reshape.19 = bf16[4,32,2,2048]{3,2,1,0:T(2,128)(2,1)} reshape(bf16[4,32,2,8,256]{4,3,2,1,0:T(8,128)(2,1)S(1)} %copy.9) | data formatting | bytes 2097152 | tf_op jit(solution)/shard_map/reshape | solution.py:281
  84.0 0.0 copy-done
  84.0 1.1 %copy.16 = f32[3,4,4,2,32,32]{5,4,3,2,1,0:T(8,128)} copy(f32[3,4,4,2,32,32]{5,4,3,2,1,0:T(8,128)S(1)} %copy-done) | data formatting | bytes 786432
Async XLA Ops:
  80.9 3.1 %copy-start = (f32[3,4,4,2,32,32]{5,4,3,2,1,0:T(8,128)S(1)}, f32[3,4,4,2,32,32]{5,4,3,2,1,0:T(8,128)}, u32[]{:S(2)}) copy-start(f32[3,4,4,2,32,32]{5,4,3,2,1,0:T(8,128)} %get-tuple-element.9) | copy-start | bytes 1179652
